TPU v7x, 32 devices: a whole 2x2x4 slice. The times are simulated.
32 devices in a mesh: group: 4 (over y, x), shard: 8 (over z, core).
Axes of the slice: x: 2, y: 2, z: 4, core: 2. Of those that a mesh axis runs over, the one named last changes fastest.
Arguments:
- entity: float32 [16384, 400], P(('group', 'shard')), may hold values from -6 to 6
- entity_state: float32 [16384], P(('group', 'shard')), may hold values from 0.1 to 10
- relation: float32 [1345, 400], replicated, may hold values from -6 to 6
- relation_state: float32 [1345], replicated, may hold values from 10 to 1000
- src_send: int32 [32, 8, 128], P(('group', 'shard')), may hold values from 0 to 511
- dst_send: int32 [32, 8, 128], P(('group', 'shard')), may hold values from 0 to 511
- edge_source: int32 [32768], P(('group', 'shard')), may hold values from 0 to 1023
- edge_relation: int32 [32768], P(('group', 'shard')), may hold values from 0 to 1344
- edge_target: int32 [32768], P(('group', 'shard')), may hold values from 0 to 1023
- neg_slots: int32 [64, 1000], P(('group', 'shard')), may hold values from 0 to 1023
- edge_count: int32 [32], P(('group', 'shard')), may hold values from 1 to 1024, 10922 in all
Outputs:
- entity_new: float32 [16384, 400], P(('group', 'shard'))
- relation_new: float32 [1345, 400], replicated
- edge_loss: float32 [32768], P(('group', 'shard'))
Inputs may be any that keep to these rules, and one draw needn't show every extreme that they name: The live edges of a device are its first edge_count slots; some device has all 1024 live.
All inputs are finite; a program needn't handle non-finite values.
Results may differ from a plain program's by a relative error of at most 0.0003.
Values sent between devices are 32-bit elements; how exact they have to be, the bound alone decides.
No kernel may reach another device: no remote copies, remote signals or barrier semaphores. Data moves between devices by JAX's collectives and lax.ppermute only.
A program may use at most 128 MiB of HBM per device.

v0:
```python
import jax
import jax.numpy as jnp
from jax import lax
from jax.sharding import PartitionSpec as P

SPAN = 512
learn_rate = 0.5


def passed_along(value, axis, by):
    count = lax.axis_size(axis)
    return lax.ppermute(value, axis, [(i, (i + by) % count) for i in range(count)])


def complex_product(multiplier, multiplicand):
    half_width = multiplier.shape[1] // 2
    first_real, first_imag = (multiplier[:, :half_width], multiplier[:, half_width:])
    second_real, second_imag = (multiplicand[:, :half_width], multiplicand[:, half_width:])
    return jnp.concatenate(
        [
            first_real * second_real - first_imag * second_imag,
            first_real * second_imag + first_imag * second_real,
        ],
        axis=1,
    )


def conj_product(multiplier, multiplicand):
    half_width = multiplier.shape[1] // 2
    first_real, first_imag = (multiplier[:, :half_width], multiplier[:, half_width:])
    second_real, second_imag = (multiplicand[:, :half_width], multiplicand[:, half_width:])
    return jnp.concatenate(
        [
            first_real * second_real + first_imag * second_imag,
            first_imag * second_real - first_real * second_imag,
        ],
        axis=1,
    )


def span_terms(queries, tail_rows, negatives, live_mask):
    pos_score = jnp.sum(queries * tail_rows, axis=1)
    neg_score = jnp.dot(queries, negatives.T, precision=lax.Precision.HIGHEST)
    score_peak = jnp.maximum(pos_score, jnp.max(neg_score, axis=1))
    exp_total = jnp.exp(pos_score - score_peak) + jnp.sum(
        jnp.exp(neg_score - score_peak[:, None]), axis=1
    )
    log_total = score_peak + jnp.log(exp_total)
    edge_loss = (log_total - pos_score) * live_mask
    pos_grad = (jnp.exp(pos_score - log_total) - 1.0) * live_mask
    neg_grad = jnp.exp(neg_score - log_total[:, None]) * live_mask[:, None]
    neg_query = jnp.dot(neg_grad, negatives, precision=lax.Precision.HIGHEST)
    negative_grad = lax.dot_general(
        neg_grad, queries, (((0,), (0,)), ((), ())), precision=lax.Precision.HIGHEST
    )
    return (edge_loss, pos_grad, neg_query, negative_grad)


def adagrad(params, accumulator, gradient):
    new_state = accumulator + jnp.mean(gradient * gradient, axis=1)
    return params - learn_rate * gradient / jnp.sqrt(new_state)[:, None]


def on_device(
    entity,
    entity_state,
    relation,
    relation_state,
    src_send,
    dst_send,
    edge_source,
    edge_relation,
    edge_target,
    neg_slots,
    edge_count,
):
    feature_count = entity.shape[1]
    peer_count, block_size = (src_send.shape[1], src_send.shape[2])
    table_rows = peer_count * block_size
    edge_rows = edge_source.shape[0]
    spans = edge_rows // SPAN
    sent_source = lax.all_to_all(
        entity[src_send[0]], "shard", split_axis=0, concat_axis=0, tiled=True
    )
    source_table = sent_source.reshape(table_rows, feature_count)
    shifted = passed_along(entity[dst_send[0]], "group", -1)
    target_blocks = lax.all_to_all(shifted, "shard", split_axis=0, concat_axis=0, tiled=True)
    target_table = target_blocks.reshape(table_rows, feature_count)
    live_count = edge_count[0]
    live_mask = (jnp.arange(edge_rows, dtype=jnp.int32) < live_count).astype(jnp.float32)
    head_rows = source_table[edge_source]
    tail_rows = target_table[edge_target]
    rel_rows = relation[edge_relation]
    queries = complex_product(head_rows, rel_rows)

    def span_turn(position, carried):
        loss_all, pos_all, query_all, target_grad = carried
        first_row = position * SPAN
        slots = neg_slots[position]
        edge_loss, pos_grad, neg_query, negative_grad = span_terms(
            lax.dynamic_slice_in_dim(queries, first_row, SPAN),
            lax.dynamic_slice_in_dim(tail_rows, first_row, SPAN),
            target_table[slots],
            lax.dynamic_slice_in_dim(live_mask, first_row, SPAN),
        )
        loss_all = lax.dynamic_update_slice_in_dim(loss_all, edge_loss, first_row, 0)
        pos_all = lax.dynamic_update_slice_in_dim(pos_all, pos_grad, first_row, 0)
        query_all = lax.dynamic_update_slice_in_dim(query_all, neg_query, first_row, 0)
        target_grad = target_grad.at[slots].add(negative_grad)
        return (loss_all, pos_all, query_all, target_grad)

    initial = (
        jnp.zeros((edge_rows,), jnp.float32),
        jnp.zeros((edge_rows,), jnp.float32),
        jnp.zeros((edge_rows, feature_count), jnp.float32),
        jnp.zeros((table_rows, feature_count), jnp.float32),
    )
    edge_loss, pos_grad, neg_query, target_grad = lax.fori_loop(0, spans, span_turn, initial)
    query_grad = pos_grad[:, None] * tail_rows + neg_query
    target_grad = target_grad.at[edge_target].add(pos_grad[:, None] * queries)
    source_grad = (
        jnp.zeros((table_rows, feature_count), jnp.float32)
        .at[edge_source]
        .add(conj_product(query_grad, rel_rows))
    )
    relation_part = (
        jnp.zeros(relation.shape, jnp.float32)
        .at[edge_relation]
        .add(conj_product(query_grad, head_rows))
    )
    relation_total = lax.psum(relation_part, ("group", "shard"))
    returned_source = lax.all_to_all(
        source_grad.reshape(peer_count, block_size, feature_count),
        "shard",
        split_axis=0,
        concat_axis=0,
        tiled=True,
    )
    entity_grad = (
        jnp.zeros(entity.shape, jnp.float32)
        .at[src_send[0].reshape(-1)]
        .add(returned_source.reshape(-1, feature_count))
    )
    target_blocks_grad = target_grad.reshape(peer_count, block_size, feature_count)
    returned_blocks = lax.all_to_all(
        target_blocks_grad, "shard", split_axis=0, concat_axis=0, tiled=True
    )
    home_blocks = passed_along(returned_blocks, "group", 1)
    entity_grad = entity_grad.at[dst_send[0].reshape(-1)].add(
        home_blocks.reshape(-1, feature_count)
    )
    return (
        adagrad(entity, entity_state, entity_grad),
        adagrad(relation, relation_state, relation_total),
        edge_loss,
    )


def solution(mesh):
    return jax.shard_map(
        on_device,
        mesh=mesh,
        in_specs=(
            P(("group", "shard"), None),
            P(("group", "shard")),
            P(),
            P(),
            P(("group", "shard"), None, None),
            P(("group", "shard"), None, None),
            P(("group", "shard")),
            P(("group", "shard")),
            P(("group", "shard")),
            P(("group", "shard"), None),
            P(("group", "shard")),
        ),
        out_specs=(P(("group", "shard"), None), P(), P(("group", "shard"))),
        check_vma=False,
    )
```

profile of v0, /device:TPU:0, one launch (start us, length us, event | category | flops | bytes accessed | tf_op | source)
XLA Modules:
  0.0 453.2 jit_solution(17644259954135910867)
XLA Ops:
  9.4 3.5 gather_fusion.1
  12.9 1.7 copy.47
  14.6 6.5 %all-to-all-start = ((f32[8,128,400]{1,2,0:T(8,128)}), f32[8,128,400]{1,2,0:T(8,128)}, u32[]{:S(2)}, u32[]{:S(2)}) async-start(f32[8,128,400]{1,2,0:T(8,128)} %copy.47), calls=%async_computation | async-start | bytes 3276800 | tf_op jit(solution)/shard_map/all_to_all | solution.py:82
  21.1 3.5 gather_fusion.4
  24.6 1.8 copy.51
  26.4 2.4 collective-permute-start
  28.8 36.1 %collective-permute-done = f32[8,128,400]{1,2,0:T(8,128)} collective-permute-done((f32[8,128,400]{1,2,0:T(8,128)}, f32[8,128,400]{1,2,0:T(8,128)}, u32[]{:S(2)}, u32[]{:S(2)}) %collective-permute-start) | collective-permute-done | bytes 1638432 | tf_op jit(solution)/shard_map/ppermute | solution.py:12
  64.9 4.7 %all-to-all-start.1 = ((f32[8,128,400]{1,2,0:T(8,128)}), f32[8,128,400]{1,2,0:T(8,128)}, u32[]{:S(2)}, u32[]{:S(2)}) async-start(f32[8,128,400]{1,2,0:T(8,128)} %collective-permute-done), calls=%async_computation.1 | async-start | bytes 3276800 | tf_op jit(solution)/shard_map/all_to_all | solution.py:87
  69.6 2.5 copy.49
  72.9 4.9 %gather_fusion.3 = f32[1024,400]{1,0:T(8,128)} fusion(f32[1345,400]{1,0:T(8,128)S(1)} %copy.49, s32[1024]{0:T(1024)S(1)} %get-tuple-element.335), kind=kCustom, calls=%fused_computation.3 | custom fusion | bytes 3280896 | tf_op jit(solution)/shard_map/gather | solution.py:93
  77.8 1.8 copy.48
  79.6 4.9 %gather_fusion.2 = f32[1024,400]{1,0:T(8,128)} fusion(f32[1024,400]{1,0:T(8,128)S(1)} %bitcast.42, s32[1024]{0:T(1024)S(1)} %get-tuple-element.338), kind=kCustom, calls=%fused_computation.2 | custom fusion | bytes 3280896 | tf_op jit(solution)/shard_map/gather | solution.py:91
  84.6 3.1 multiply_subtract_fusion.2
  88.7 1.8 pad_maximum_fusion
  90.5 18.4 %all-to-all-done.1 = f32[8,128,400]{1,2,0:T(8,128)} async-done(((f32[8,128,400]{1,2,0:T(8,128)}), f32[8,128,400]{1,2,0:T(8,128)}, u32[]{:S(2)}, u32[]{:S(2)}) %all-to-all-start.1) | async-done | bytes 1638432 | tf_op jit(solution)/shard_map/all_to_all | solution.py:87
  108.9 1.8 copy.52
  110.8 4.9 %gather_fusion.5 = f32[1024,400]{1,0:T(8,128)} fusion(f32[1024,400]{1,0:T(8,128)S(1)} %bitcast.39, s32[1024]{0:T(1024)S(1)} %get-tuple-element.337), kind=kCustom, calls=%fused_computation.5 | custom fusion | bytes 3280896 | tf_op jit(solution)/shard_map/gather | solution.py:92
  118.7 68.8 %while.21 = (s32[]{:T(128)}, f32[1024]{0:T(1024)S(1)}, f32[1024]{0:T(1024)S(1)}, f32[1024,400]{0,1:T(8,128)}, f32[1024,400]{1,0:T(8,128)}, /*index=5*/f32[1024,4...) while((s32[]{:T(128)}, f32[1024]{0:T(1024)S(1)}, ...), condition=%wide.region_5.0_spmd, body=%wide.region_0.0_spmd.sunk | while | flops 7377200640 | bytes 52573032 | solution.py:118
  120.9 4.9 %gather_fusion = f32[1000,400]{1,0:T(8,128)} fusion(f32[1024,400]{1,0:T(8,128)S(1)} %get-tuple-element.447, s32[1024]{0:T(1024)S(1)} %pad_clamp_fusion.2), kind=kCustom, calls=%fused_computation.clone.1 | custom fusion | bytes 3204000 | tf_op jit(solution)/shard_map/while/body/eval_jaxpr/gather | solution.py:103
  125.8 5.4 %fusion.44 = (f32[512]{0:T(512)S(1)}, f32[512,1000]{0,1:T(8,128)S(1)}) fusion(f32[1000,400]{1,0:T(8,128)} %gather_fusion, f32[1024,400]{1,0:T(8,128)} %get-tuple-element.444, s32[]{:T(128)S(6)} %select_n.125), kind=kOutput, calls=%fused_computation.77.clone.1 | convolution fusion | flops 2458111488 | bytes 5146628 | tf_op jit(solution)/shard_map/while/body/eval_jaxpr/dot_general | solution.py:43
  132.8 4.2 fusion.45
  138.3 4.9 %fusion.46 = f32[1000,400]{1,0:T(8,128)} fusion(f32[512,1000]{0,1:T(8,128)S(1)} %get-tuple-element.407, f32[512]{0:T(512)S(1)} %get-tuple-element.408, f32[512]{0:T(512)S(1)} %get-tuple-element.409, f32[1024,400]{1,0:T(8,128)S(1)} %copy-done.5, s32[]{:T(128)S(6)} %select_n.125), kind=kOutput, calls=%fused_computation.14.clone.1 | convolution fusion | flops 2458624000 | bytes 4700676 | tf_op jit(solution)/shard_map/while/body/eval_jaxpr/dot_general | solution.py:53
  143.2 10.1 %scatter_fusion = f32[1024,400]{1,0:T(8,128)} fusion(f32[1024,400]{1,0:T(8,128)} %get-tuple-element.429, s32[1000]{0:T(1024)S(1)} %bitcast.49, f32[1000,400]{1,0:T(8,128)} %fusion.46), kind=kCustom, calls=%fused_computation.6.clone.1 | custom fusion | flops 400000 | bytes 4804000 | tf_op jit(solution)/shard_map/while/body/eval_jaxpr/scatter-add | solution.py:109
  155.0 4.9 %gather_fusion = f32[1000,400]{1,0:T(8,128)} fusion(f32[1024,400]{1,0:T(8,128)S(1)} %get-tuple-element.447, s32[1024]{0:T(1024)S(1)} %pad_clamp_fusion.2), kind=kCustom, calls=%fused_computation.clone.1 | custom fusion | bytes 3204000 | tf_op jit(solution)/shard_map/while/body/eval_jaxpr/gather | solution.py:103
  159.9 5.4 %fusion.44 = (f32[512]{0:T(512)S(1)}, f32[512,1000]{0,1:T(8,128)S(1)}) fusion(f32[1000,400]{1,0:T(8,128)} %gather_fusion, f32[1024,400]{1,0:T(8,128)} %get-tuple-element.444, s32[]{:T(128)S(6)} %select_n.125), kind=kOutput, calls=%fused_computation.77.clone.1 | convolution fusion | flops 2458111488 | bytes 5146628 | tf_op jit(solution)/shard_map/while/body/eval_jaxpr/dot_general | solution.py:43
  166.9 4.2 fusion.45
  172.4 4.9 %fusion.46 = f32[1000,400]{1,0:T(8,128)} fusion(f32[512,1000]{0,1:T(8,128)S(1)} %get-tuple-element.407, f32[512]{0:T(512)S(1)} %get-tuple-element.408, f32[512]{0:T(512)S(1)} %get-tuple-element.409, f32[1024,400]{1,0:T(8,128)S(1)} %copy-done.5, s32[]{:T(128)S(6)} %select_n.125), kind=kOutput, calls=%fused_computation.14.clone.1 | convolution fusion | flops 2458624000 | bytes 4700676 | tf_op jit(solution)/shard_map/while/body/eval_jaxpr/dot_general | solution.py:53
  177.2 10.1 %scatter_fusion = f32[1024,400]{1,0:T(8,128)} fusion(f32[1024,400]{1,0:T(8,128)} %get-tuple-element.429, s32[1000]{0:T(1024)S(1)} %bitcast.49, f32[1000,400]{1,0:T(8,128)} %fusion.46), kind=kCustom, calls=%fused_computation.6.clone.1 | custom fusion | flops 400000 | bytes 4804000 | tf_op jit(solution)/shard_map/while/body/eval_jaxpr/scatter-add | solution.py:109
  187.5 10.6 %scatter_custom_fusion.3 = f32[1024,400]{1,0:T(8,128)} fusion(f32[1024,400]{1,0:T(8,128)} %get-tuple-element.250, s32[1024]{0:T(1024)S(1)} %get-tuple-element.336, f32[1024]{0:T(1024)S(1)} %get-tuple-element.248, f32[1024,200]{1,0:T(8,128)} %copy-done.9, f32[1024,200]{1,0:T(8,128)S(1)} %get-tuple-element.330), kind=kCustom, calls=%fused_computation.43 | custom fusion | flops 1228800 | bytes 3739648 | tf_op jit(solution)/shard_map/scatter-add | solution.py:120
  198.1 2.8 copy.59
  200.9 4.3 all-to-all-start.3
  205.2 3.0 copy.54
  208.2 2.0 multiply_add_fusion
  211.0 2.5 multiply_add_fusion.1
  213.6 8.1 %scatter_custom_fusion.1 = f32[1024,400]{1,0:T(8,128)S(1)} fusion(s32[1024]{0:T(1024)S(1)} %get-tuple-element.339, f32[1024,200]{1,0:T(8,128)S(1)} %get-tuple-element.332, f32[]{:T(128)} %constant.108, f32[1024,200]{1,0:T(8,128)} %get-tuple-element.333, f32[]{:T(128)} %constant.97.clone.1), kind=kCustom, calls=%fused_computation.35 | custom fusion | flops 819200 | bytes 3506184 | tf_op jit(solution)/shard_map/scatter-add | solution.py:124
  221.7 1.7 copy.55
  223.5 21.0 %all-to-all-done.3 = f32[8,128,400]{1,2,0:T(8,128)} async-done(((f32[8,128,400]{1,2,0:T(8,128)}), f32[8,128,400]{1,2,0:T(8,128)}, u32[]{:S(2)}, u32[]{:S(2)}) %all-to-all-start.3) | async-done | bytes 1638432 | tf_op jit(solution)/shard_map/all_to_all | solution.py:145
  244.4 4.3 all-to-all-start.2
  248.8 9.0 %scatter_custom_fusion.5 = f32[1345,400]{1,0:T(8,128)} fusion(s32[1024]{0:T(1024)S(1)} %get-tuple-element.334, f32[1024,200]{1,0:T(8,128)S(1)} %copy-done.13, f32[]{:T(128)} %constant.108, f32[1024,200]{1,0:T(8,128)S(1)} %copy-done.12, f32[]{:T(128)} %constant.97.clone.1), kind=kCustom, calls=%fused_computation.39 | custom fusion | flops 819200 | bytes 4249160 | tf_op jit(solution)/shard_map/scatter-add | solution.py:129
  257.8 2.4 collective-permute-start.1
  260.3 155.8 %all-reduce.2.cloned.1.call-done = f32[1345,400]{1,0:T(8,128)} async-done(((f32[1345,400]{1,0:T(8,128)}), f32[1345,400]{1,0:T(8,128)}) %all-reduce.2.cloned.1.call-update) | async-done | bytes 2152016 | tf_op jit(solution)/shard_map/psum | solution.py:131
  416.1 2.1 multiply_reduce_fusion.1
  418.2 3.8 divide_subtract_fusion
  422.0 3.3 copy.65
  425.3 1.8 copy.67
  427.1 6.8 %scatter_custom_fusion.2 = f32[512,400]{1,0:T(8,128)S(1)} fusion(s32[1024]{0:T(1024)S(1)} %bitcast.53, f32[1024,400]{1,0:T(8,128)S(1)} %bitcast.47, f32[]{:T(128)} %constant.97.clone.1), kind=kCustom, calls=%fused_computation.57 | custom fusion | flops 409600 | bytes 819204 | tf_op jit(solution)/shard_map/scatter-add | solution.py:142
  434.0 2.8 copy.70
  436.8 7.8 %scatter_fusion.1 = f32[512,400]{1,0:T(8,128)S(1)} fusion(f32[512,400]{1,0:T(8,128)S(1)} %scatter_custom_fusion.2, s32[1024]{0:T(1024)S(1)} %bitcast.50, f32[1024,400]{1,0:T(8,128)} %bitcast.43), kind=kCustom, calls=%fused_computation.10 | custom fusion | flops 409600 | bytes 4919296 | tf_op jit(solution)/shard_map/scatter-add | solution.py:149
  (91 shorter events, 18.0 us)
Async XLA Ops:
  8.6 12.5 %copy-start = (f32[512,400]{1,0:T(8,128)}, f32[512,400]{1,0:T(8,128)S(1)}, u32[]{:S(2)}) copy-start(f32[512,400]{1,0:T(8,128)S(1)} %copy.62) | copy-start | bytes 2457604
  14.6 6.5 %copy-start.16 = (s32[1,8,128]{2,1,0:T(8,128)S(1)}, s32[1,8,128]{2,1,0:T(8,128)}, u32[]{:S(2)}) copy-start(s32[1,8,128]{2,1,0:T(8,128)} %param.18) | copy-start | bytes 12292
  14.6 50.3 %all-to-all-start = ((f32[8,128,400]{1,2,0:T(8,128)}), f32[8,128,400]{1,2,0:T(8,128)}, u32[]{:S(2)}, u32[]{:S(2)}) async-start(f32[8,128,400]{1,2,0:T(8,128)} %copy.47), calls=%async_computation | async-start | bytes 3276800 | tf_op jit(solution)/shard_map/all_to_all | solution.py:82
  26.4 38.5 %collective-permute-start = (f32[8,128,400]{1,2,0:T(8,128)}, f32[8,128,400]{1,2,0:T(8,128)}, u32[]{:S(2)}, u32[]{:S(2)}) collective-permute-start(f32[8,128,400]{1,2,0:T(8,128)} %copy.51), channel_id=1, source_target_pairs={{0,24},{8,0},{16,8},{24,16},{1,25},{9,1},{17,9},{25,17},{2,26},{10... | collective-permute-start | bytes 4915208 | tf_op jit(solution)/shard_map/ppermute | solution.py:12
  64.9 44.0 %all-to-all-start.1 = ((f32[8,128,400]{1,2,0:T(8,128)}), f32[8,128,400]{1,2,0:T(8,128)}, u32[]{:S(2)}, u32[]{:S(2)}) async-start(f32[8,128,400]{1,2,0:T(8,128)} %collective-permute-done), calls=%async_computation.1 | async-start | bytes 3276800 | tf_op jit(solution)/shard_map/all_to_all | solution.py:87
  69.6 3.2 copy-start.18
  72.1 5.6 %copy-start.3 = (f32[1345,400]{1,0:T(8,128)}, f32[1345,400]{1,0:T(8,128)S(1)}, u32[]{:S(2)}) copy-start(f32[1345,400]{1,0:T(8,128)S(1)} %copy.49) | copy-start | bytes 6456004
  72.8 4.9 %copy-start.19 = (s32[1024]{0:T(1024)S(1)}, s32[1024]{0:T(1024)}, u32[]{:S(2)}) copy-start(s32[1024]{0:T(1024)} %param.19) | copy-start | bytes 12292
  72.8 4.9 %copy-start.20 = (s32[1024]{0:T(1024)S(1)}, s32[1024]{0:T(1024)}, u32[]{:S(2)}) copy-start(s32[1024]{0:T(1024)} %param.21) | copy-start | bytes 12292
  87.7 1.0 copy-start.9
  115.6 3.1 copy-start.14
  125.8 6.1 %copy-start.10 = (f32[1024,400]{0,1:T(8,128)S(1)}, f32[1024,400]{0,1:T(8,128)}, u32[]{:S(2)}) copy-start(f32[1024,400]{0,1:T(8,128)} %get-tuple-element.428) | copy-start | bytes 4915204 | tf_op jit(solution)/shard_map/while
  131.2 1.6 copy-start.2
  132.8 5.5 %copy-start.5 = (f32[1024,400]{1,0:T(8,128)S(1)}, f32[1024,400]{1,0:T(8,128)}, u32[]{:S(2)}) copy-start(f32[1024,400]{1,0:T(8,128)} %get-tuple-element.444) | copy-start | bytes 4915204 | tf_op jit(solution)/shard_map/while
  137.0 1.3 copy-start.11
  159.9 6.1 %copy-start.10 = (f32[1024,400]{0,1:T(8,128)S(1)}, f32[1024,400]{0,1:T(8,128)}, u32[]{:S(2)}) copy-start(f32[1024,400]{0,1:T(8,128)} %get-tuple-element.428) | copy-start | bytes 4915204 | tf_op jit(solution)/shard_map/while
  165.3 1.6 copy-start.2
  166.9 5.5 %copy-start.5 = (f32[1024,400]{1,0:T(8,128)S(1)}, f32[1024,400]{1,0:T(8,128)}, u32[]{:S(2)}) copy-start(f32[1024,400]{1,0:T(8,128)} %get-tuple-element.444) | copy-start | bytes 4915204 | tf_op jit(solution)/shard_map/while
  171.1 1.3 copy-start.11
  187.5 10.6 %copy-start.21 = (f32[1024]{0:T(1024)}, f32[1024]{0:T(1024)S(1)}, u32[]{:S(2)}) copy-start(f32[1024]{0:T(1024)S(1)} %get-tuple-element.300) | copy-start | bytes 12292
  200.9 43.5 %all-to-all-start.3 = ((f32[8,128,400]{1,2,0:T(8,128)}), f32[8,128,400]{1,2,0:T(8,128)}, u32[]{:S(2)}, u32[]{:S(2)}) async-start(f32[8,128,400]{1,2,0:T(8,128)} %copy.59), calls=%async_computation.3 | async-start | bytes 3276800 | tf_op jit(solution)/shard_map/all_to_all | solution.py:145
  205.2 3.0 copy-start.6
  208.2 2.2 copy-start.7
  208.2 2.9 copy-start.8
  223.5 25.3 %copy-start.12 = (f32[1024,200]{1,0:T(8,128)S(1)}, f32[1024,200]{1,0:T(8,128)}, u32[]{:S(2)}) copy-start(f32[1024,200]{1,0:T(8,128)} %get-tuple-element.326) | copy-start | bytes 2457604
  223.5 25.3 %copy-start.13 = (f32[1024,200]{1,0:T(8,128)S(1)}, f32[1024,200]{1,0:T(8,128)}, u32[]{:S(2)}) copy-start(f32[1024,200]{1,0:T(8,128)} %get-tuple-element.327) | copy-start | bytes 2457604
  244.4 180.8 %all-to-all-start.2 = ((f32[8,128,400]{1,2,0:T(8,128)}), f32[8,128,400]{1,2,0:T(8,128)}, u32[]{:S(2)}, u32[]{:S(2)}) async-start(f32[8,128,400]{1,2,0:T(8,128)} %copy.55), calls=%async_computation.2 | async-start | bytes 3276800 | tf_op jit(solution)/shard_map/all_to_all | solution.py:132
  248.7 167.4 %all-reduce.2.cloned.1.call-start = ((), (), s32[]{:S(2)}) async-start(), calls=%async_computation.4 | async-start | bytes 5537792 | tf_op jit(solution)/shard_map/psum | solution.py:131
  257.8 2.5 copy-start.15
  257.8 160.4 %copy-start.17 = (f32[1345]{0:T(1024)S(1)}, f32[1345]{0:T(1024)}, u32[]{:S(2)}) copy-start(f32[1345]{0:T(1024)} %param.16) | copy-start | bytes 16144
  257.8 160.4 %copy-start.4 = (f32[1345,400]{1,0:T(8,128)S(1)}, f32[1345,400]{1,0:T(8,128)}, u32[]{:S(2)}) copy-start(f32[1345,400]{1,0:T(8,128)} %copy-done.3) | copy-start | bytes 6456004
  257.8 176.1 %collective-permute-start.1 = (f32[8,128,400]{1,2,0:T(8,128)}, f32[8,128,400]{1,2,0:T(8,128)}, u32[]{:S(2)}, u32[]{:S(2)}) collective-permute-start(f32[8,128,400]{1,2,0:T(8,128)} %all-to-all-done.3), channel_id=1, source_target_pairs={{0,8},{8,16},{16,24},{24,0},{1,9},{9,17},{17,25},{25,1},{2,10},{10... | collective-permute-start | bytes 4915208 | tf_op jit(solution)/shard_map/ppermute | solution.py:12
  436.8 7.9 %copy-start.22 = (f32[512]{0:T(512)S(1)}, f32[512]{0:T(512)}, u32[]{:S(2)}) copy-start(f32[512]{0:T(512)} %param.14) | copy-start | bytes 6148
  436.8 7.9 %copy-start.1 = (f32[512,400]{1,0:T(8,128)S(1)}, f32[512,400]{1,0:T(8,128)}, u32[]{:S(2)}) copy-start(f32[512,400]{1,0:T(8,128)} %copy-done) | copy-start | bytes 2457604
Sparse Core Ops, SparseCore 0:
  257.9 158.1 all-reduce.1
where the time goes:
time: 458 us; the launch traced here: 453 us
  waiting for transfers between devices  231 us (50%)
  other arithmetic  83.6 us (18%)
  local copies, waits for them, and re-layouts  68.6 us (15%)
  matrix products  29 us (6%)
  starting transfers between devices  24.7 us (5%)
  between operations  15.3 us (3%)
    psum x1, waiting for transfers between devices, on_device(): relation_total = lax.psum(relation_part, ('group', 'shard'))  156 us
    ppermute x2, waiting for transfers between devices, passed_along(): lax.ppermute(value, axis, [(i, (i + by) % count) for i in range(count)])  36.1 us
    all_to_all x1, waiting for transfers between devices, on_device(): lax.all_to_all(target_blocks_grad, 'shard', split_axis=0, concat_axis=0,...  21 us
    scatter-add x2, other arithmetic, span_turn(): target_grad = target_grad.at[slots].add(negative_grad)  20.2 us
    all_to_all x1, waiting for transfers between devices, on_device(): lax.all_to_all(shifted, 'shard', split_axis=0, concat_axis=0, tiled=True)  18.4 us
    dot_general x2, matrix products, span_terms(): neg_score = jnp.dot(queries, negatives.T, precision=lax.Precision.HIGHEST)  10.9 us
    scatter-add x1, other arithmetic, on_device(): target_grad = target_grad.at[edge_target].add(pos_grad[:, None] * queries)  10.6 us
    unnamed x42, local copies, waits for them, and re-layouts  10.4 us
  transfers between devices with their start and end apart: 7, of which 4 were waited for; matrix products, arithmetic and copies ran while one was open for 15% of the time, Pallas kernels for 0%

commit v1 on v0

--- a/solution.py
+++ b/solution.py
@@ -5,6 +5,7 @@
 
 SPAN = 512
 learn_rate = 0.5
+follow_panels = lambda v0: jnp.sum(lax.all_gather(v0, axis_name=("group", "shard")), axis=0)
 
 
 def passed_along(value, axis, by):
@@ -128,7 +129,7 @@
         .at[edge_relation]
         .add(conj_product(query_grad, head_rows))
     )
-    relation_total = lax.psum(relation_part, ("group", "shard"))
+    relation_total = follow_panels(relation_part)
     returned_source = lax.all_to_all(
         source_grad.reshape(peer_count, block_size, feature_count),
         "shard",

time: 458 us -> 692 us (1.51)
  waiting for transfers between devices: 231 us -> 449 us
  other arithmetic: 83.6 us -> 100 us
    all_gather x0 -> x1, waiting for transfers between devices: none -> 249 us  [lax.all_gather(v0, axis_name=('group', 'shard'))]
    psum x1 -> x0, waiting for transfers between devices: 156 us -> none  [on_device(): relation_total = lax.psum(relation_part, ('group', 'shard'))]
    all_to_all x1, waiting for transfers between devices: 0.01 us -> 77.7 us  [on_device(): lax.all_to_all(source_grad.reshape(peer_count, block_size, feature_count)...]
    all_to_all x1, waiting for transfers between devices: 21 us -> 68.1 us  [on_device(): lax.all_to_all(target_blocks_grad, 'shard', split_axis=0, concat_axis=0,...]
    reduce_sum x0 -> x1, other arithmetic: none -> 22.3 us  [jnp.sum(lax.all_gather(v0, axis_name=('group', 'shard')), axis=0)]
  transfers between devices with their start and end apart: 7 -> 7, of which waited for: 4 -> 5; matrix products, arithmetic and copies ran while one was open for 15% -> 9% of each run, Pallas kernels for 0% -> 0%
where the time goes in v1:
time: 692 us; the launch traced here: 687 us
  waiting for transfers between devices  449 us (65%)
  other arithmetic  100 us (14%)
  local copies, waits for them, and re-layouts  68.6 us (10%)
  matrix products  29 us (4%)
  starting transfers between devices  23.7 us (3%)
  between operations  15.3 us (2%)
    all_gather x1, waiting for transfers between devices, lax.all_gather(v0, axis_name=('group', 'shard'))  249 us
    all_to_all x1, waiting for transfers between devices, on_device(): lax.all_to_all(source_grad.reshape(peer_count, block_size, feature_count)...  77.7 us
    all_to_all x1, waiting for transfers between devices, on_device(): lax.all_to_all(target_blocks_grad, 'shard', split_axis=0, concat_axis=0,...  68.1 us
    ppermute x2, waiting for transfers between devices, passed_along(): lax.ppermute(value, axis, [(i, (i + by) % count) for i in range(count)])  36.1 us
    reduce_sum x1, other arithmetic, jnp.sum(lax.all_gather(v0, axis_name=('group', 'shard')), axis=0)  22.3 us
    scatter-add x2, other arithmetic, span_turn(): target_grad = target_grad.at[slots].add(negative_grad)  20.3 us
    all_to_all x1, waiting for transfers between devices, on_device(): lax.all_to_all(shifted, 'shard', split_axis=0, concat_axis=0, tiled=True)  18.1 us
  transfers between devices with their start and end apart: 7, of which 5 were waited for; matrix products, arithmetic and copies ran while one was open for 9% of the time, Pallas kernels for 0%

profile of v1, /device:TPU:0, one launch (start us, length us, event | category | flops | bytes accessed | tf_op | source)
XLA Modules:
  0.0 686.9 jit_solution(15464881955999056468)
XLA Ops:
  9.4 3.5 gather_fusion.1
  12.9 1.7 copy.43
  14.6 6.5 all-to-all-start
  21.1 3.5 gather_fusion.4
  24.6 1.8 copy.47
  26.4 2.4 collective-permute-start
  28.8 36.1 %collective-permute-done = f32[8,128,400]{1,2,0:T(8,128)} collective-permute-done((f32[8,128,400]{1,2,0:T(8,128)}, f32[8,128,400]{1,2,0:T(8,128)}, u32[]{:S(2)}, u32[]{:S(2)}) %collective-permute-start) | collective-permute-done | bytes 1638432 | tf_op jit(solution)/shard_map/ppermute | solution.py:13
  64.9 4.7 all-to-all-start.1
  69.7 2.5 copy.45
  72.9 4.9 gather_fusion.3
  77.8 1.8 copy.44
  79.7 4.9 gather_fusion.2
  84.5 3.1 multiply_subtract_fusion.2
  89.0 1.8 pad_maximum_fusion
  90.8 18.1 %all-to-all-done.1 = f32[8,128,400]{1,2,0:T(8,128)} async-done(((f32[8,128,400]{1,2,0:T(8,128)}), f32[8,128,400]{1,2,0:T(8,128)}, u32[]{:S(2)}, u32[]{:S(2)}) %all-to-all-start.1) | async-done | bytes 1638432 | tf_op jit(solution)/shard_map/all_to_all | solution.py:88
  108.9 1.8 copy.48
  110.8 4.9 gather_fusion.5
  118.8 68.8 %while.21 = (s32[]{:T(128)}, f32[1024]{0:T(1024)S(1)}, f32[1024]{0:T(1024)S(1)}, f32[1024,400]{0,1:T(8,128)}, f32[1024,400]{1,0:T(8,128)}, /*index=5*/f32[1024,4...) while((s32[]{:T(128)}, f32[1024]{0:T(1024)S(1)}, ...), condition=%wide.region_5.0_spmd, body=%wide.region_0.0_spmd.sunk | while | flops 7377200640 | bytes 52573032 | solution.py:119
  121.0 4.9 gather_fusion
  125.9 5.4 fusion.44
  132.9 4.2 fusion.45
  138.4 4.9 fusion.46
  143.2 10.1 %scatter_fusion = f32[1024,400]{1,0:T(8,128)} fusion(f32[1024,400]{1,0:T(8,128)} %get-tuple-element.429, s32[1000]{0:T(1024)S(1)} %bitcast.51, f32[1000,400]{1,0:T(8,128)} %fusion.46), kind=kCustom, calls=%fused_computation.6.clone.1 | custom fusion | flops 400000 | bytes 4804000 | tf_op jit(solution)/shard_map/while/body/eval_jaxpr/scatter-add | solution.py:110
  155.1 4.9 gather_fusion
  160.0 5.4 fusion.44
  167.0 4.2 fusion.45
  172.5 4.9 fusion.46
  177.3 10.1 %scatter_fusion = f32[1024,400]{1,0:T(8,128)} fusion(f32[1024,400]{1,0:T(8,128)} %get-tuple-element.429, s32[1000]{0:T(1024)S(1)} %bitcast.51, f32[1000,400]{1,0:T(8,128)} %fusion.46), kind=kCustom, calls=%fused_computation.6.clone.1 | custom fusion | flops 400000 | bytes 4804000 | tf_op jit(solution)/shard_map/while/body/eval_jaxpr/scatter-add | solution.py:110
  187.6 3.0 copy.50
  190.6 2.0 multiply_add_fusion
  193.5 2.9 multiply_add_fusion.1
  196.3 8.4 %scatter_custom_fusion.5 = f32[1345,400]{1,0:T(8,128)S(1)} fusion(s32[1024]{0:T(1024)S(1)} %get-tuple-element.334, f32[1024,200]{1,0:T(8,128)} %get-tuple-element.327, f32[]{:T(128)} %constant.108, f32[1024,200]{1,0:T(8,128)} %get-tuple-element.326, f32[]{:T(128)} %constant.97.clone.1), kind=kCustom, calls=%fused_computation.39 | custom fusion | flops 819200 | bytes 3790408 | tf_op jit(solution)/shard_map/scatter-add | solution.py:130
  204.8 2.1 copy.59
  208.5 8.7 %scatter_custom_fusion.3 = f32[1024,400]{1,0:T(8,128)S(1)} fusion(f32[1024,400]{1,0:T(8,128)S(1)} %copy-done, s32[1024]{0:T(1024)S(1)} %get-tuple-element.336, f32[1024]{0:T(1024)S(1)} %get-tuple-element.248, f32[1024,200]{1,0:T(8,128)} %copy-done.9, f32[1024,200]{1,0:T(8,128)} %copy-done.8), kind=kCustom, calls=%fused_computation.43 | custom fusion | flops 1228800 | bytes 3280896 | tf_op jit(solution)/shard_map/scatter-add | solution.py:121
  217.2 1.7 copy.55
  218.9 4.6 all-to-all-start.3
  223.5 8.1 %scatter_custom_fusion.1 = f32[1024,400]{1,0:T(8,128)S(1)} fusion(s32[1024]{0:T(1024)S(1)} %get-tuple-element.339, f32[1024,200]{1,0:T(8,128)S(1)} %copy-done.13, f32[]{:T(128)} %constant.108, f32[1024,200]{1,0:T(8,128)} %get-tuple-element.333, f32[]{:T(128)} %constant.97.clone.1), kind=kCustom, calls=%fused_computation.35 | custom fusion | flops 819200 | bytes 3506184 | tf_op jit(solution)/shard_map/scatter-add | solution.py:125
  231.7 1.8 copy.51
  233.5 68.1 %all-to-all-done.3 = f32[8,128,400]{1,2,0:T(8,128)} async-done(((f32[8,128,400]{1,2,0:T(8,128)}), f32[8,128,400]{1,2,0:T(8,128)}, u32[]{:S(2)}, u32[]{:S(2)}) %all-to-all-start.3) | async-done | bytes 1638432 | tf_op jit(solution)/shard_map/all_to_all | solution.py:146
  301.5 3.6 all-to-all-start.2
  305.1 1.8 collective-permute-start.1
  306.9 77.7 %all-to-all-done.2 = f32[8,128,400]{1,2,0:T(8,128)S(1)} async-done(((f32[8,128,400]{1,2,0:T(8,128)}), f32[8,128,400]{1,2,0:T(8,128)S(1)}, u32[]{:S(2)}, u32[]{:S(2)}) %all-to-all-start.2) | async-done | bytes 1638432 | tf_op jit(solution)/shard_map/all_to_all | solution.py:133
  384.7 1.8 copy.62
  386.4 7.5 %scatter_custom_fusion.2 = f32[512,400]{1,0:T(8,128)S(1)} fusion(s32[1024]{0:T(1024)S(1)} %bitcast.55, f32[1024,400]{1,0:T(8,128)} %bitcast.49, f32[]{:T(128)} %constant.97.clone.1), kind=kCustom, calls=%fused_computation.57 | custom fusion | flops 409600 | bytes 819712 | tf_op jit(solution)/shard_map/scatter-add | solution.py:143
  394.0 1.8 copy.65
  395.8 7.8 %scatter_fusion.1 = f32[512,400]{1,0:T(8,128)S(1)} fusion(f32[512,400]{1,0:T(8,128)S(1)} %scatter_custom_fusion.2, s32[1024]{0:T(1024)S(1)} %bitcast.52, f32[1024,400]{1,0:T(8,128)} %bitcast.45), kind=kCustom, calls=%fused_computation.10 | custom fusion | flops 409600 | bytes 4919296 | tf_op jit(solution)/shard_map/scatter-add | solution.py:150
  405.1 249.1 %all-gather.4.cloned.1.call-done = f32[32,1345,400]{1,2,0:T(8,128)} async-done(((f32[1,1345,400]{1,2,0:T(8,128)}), f32[32,1345,400]{1,2,0:T(8,128)}) %all-gather.4.cloned.1.call-update) | async-done | bytes 68864016 | tf_op jit(solution)/shard_map/all_gather | solution.py:8
  654.3 22.3 %reduce_sum.60 = f32[1345,400]{0,1:T(8,128)S(1)} reduce(f32[32,1345,400]{1,2,0:T(8,128)} %all-gather.4.cloned.1.call-done, f32[]{:T(128)} %constant.97.clone.1), dimensions={0}, to_apply=%region_12.0 | reduce | flops 16678000 | bytes 71016000 | tf_op jit(solution)/shard_map/reduce_sum | solution.py:8
  (92 shorter events, 23.0 us)
Async XLA Ops:
  8.6 12.5 %copy-start.1 = (f32[512,400]{1,0:T(8,128)}, f32[512,400]{1,0:T(8,128)S(1)}, u32[]{:S(2)}) copy-start(f32[512,400]{1,0:T(8,128)S(1)} %copy.58) | copy-start | bytes 2457604
  14.6 6.5 copy-start.16
  14.6 50.3 %all-to-all-start = ((f32[8,128,400]{1,2,0:T(8,128)}), f32[8,128,400]{1,2,0:T(8,128)}, u32[]{:S(2)}, u32[]{:S(2)}) async-start(f32[8,128,400]{1,2,0:T(8,128)} %copy.43), calls=%async_computation | async-start | bytes 3276800 | tf_op jit(solution)/shard_map/all_to_all | solution.py:83
  26.4 38.5 %collective-permute-start = (f32[8,128,400]{1,2,0:T(8,128)}, f32[8,128,400]{1,2,0:T(8,128)}, u32[]{:S(2)}, u32[]{:S(2)}) collective-permute-start(f32[8,128,400]{1,2,0:T(8,128)} %copy.47), channel_id=1, source_target_pairs={{0,24},{8,0},{16,8},{24,16},{1,25},{9,1},{17,9},{25,17},{2,26},{10... | collective-permute-start | bytes 4915208 | tf_op jit(solution)/shard_map/ppermute | solution.py:13
  64.9 44.0 %all-to-all-start.1 = ((f32[8,128,400]{1,2,0:T(8,128)}), f32[8,128,400]{1,2,0:T(8,128)}, u32[]{:S(2)}, u32[]{:S(2)}) async-start(f32[8,128,400]{1,2,0:T(8,128)} %collective-permute-done), calls=%async_computation.1 | async-start | bytes 3276800 | tf_op jit(solution)/shard_map/all_to_all | solution.py:88
  69.6 584.6 %all-gather.4.cloned.1.call-start = ((), (), s32[]{:S(2)}) async-start(), calls=%async_computation.4 | async-start | bytes 74342400 | tf_op jit(solution)/shard_map/all_gather | solution.py:8
  69.7 3.2 copy-start.18
  72.9 4.9 copy-start.19
  72.9 4.9 copy-start.20
  87.7 1.0 copy-start.8
  87.7 1.3 copy-start.9
  115.7 3.1 copy-start.14
  125.9 6.1 copy-start.11
  131.3 1.6 copy-start.3
  132.9 5.5 copy-start.4
  137.1 1.2 copy-start.12
  160.0 6.1 copy-start.11
  165.4 1.6 copy-start.3
  167.0 5.5 copy-start.4
  171.2 1.2 copy-start.12
  187.6 5.0 copy-start.21
  187.6 3.0 copy-start.5
  190.6 2.2 copy-start.6
  190.6 2.9 copy-start.7
  206.9 1.6 copy-start
  218.9 4.7 copy-start.13
  218.9 82.6 %all-to-all-start.3 = ((f32[8,128,400]{1,2,0:T(8,128)}), f32[8,128,400]{1,2,0:T(8,128)}, u32[]{:S(2)}, u32[]{:S(2)}) async-start(f32[8,128,400]{1,2,0:T(8,128)} %copy.55), calls=%async_computation.3 | async-start | bytes 3276800 | tf_op jit(solution)/shard_map/all_to_all | solution.py:146
  233.4 73.4 %copy-start.15 = (s32[1,8,128]{2,1,0:T(8,128)S(1)}, s32[1,8,128]{2,1,0:T(8,128)}, u32[]{:S(2)}) copy-start(s32[1,8,128]{2,1,0:T(8,128)} %param.17) | copy-start | bytes 12292
  301.5 83.1 %all-to-all-start.2 = ((f32[8,128,400]{1,2,0:T(8,128)}), f32[8,128,400]{1,2,0:T(8,128)S(1)}, u32[]{:S(2)}, u32[]{:S(2)}) async-start(f32[8,128,400]{1,2,0:T(8,128)} %copy.51), calls=%async_computation.2 | async-start | bytes 3276800 | tf_op jit(solution)/shard_map/all_to_all | solution.py:133
  305.1 88.9 %collective-permute-start.1 = (f32[8,128,400]{1,2,0:T(8,128)}, f32[8,128,400]{1,2,0:T(8,128)S(1)}, u32[]{:S(2)}, u32[]{:S(2)}) collective-permute-start(f32[8,128,400]{1,2,0:T(8,128)} %all-to-all-done.3), channel_id=1, source_target_pairs={{0,8},{8,16},{16,24},{24,0},{1,9},{9,17},{17,25},{25,1},{2,10},{10... | collective-permute-start | bytes 4915208 | tf_op jit(solution)/shard_map/ppermute | solution.py:13
  395.8 7.9 %copy-start.22 = (f32[512]{0:T(512)S(1)}, f32[512]{0:T(512)}, u32[]{:S(2)}) copy-start(f32[512]{0:T(512)} %param.14) | copy-start | bytes 6148
  395.8 7.9 %copy-start.2 = (f32[512,400]{1,0:T(8,128)S(1)}, f32[512,400]{1,0:T(8,128)}, u32[]{:S(2)}) copy-start(f32[512,400]{1,0:T(8,128)} %copy-done.1) | copy-start | bytes 2457604
  676.5 0.7 copy-start.17
  676.6 1.6 copy-start.10
Sparse Core Ops, SparseCore 0:
  207.0 447.1 all-gather.3
